TPU v7x, 32 devices: a whole 2x2x4 slice. The times are simulated.
32 devices in a mesh: band: 4 (over z), roster: 8 (over y, x, core).
Axes of the slice: x: 2, y: 2, z: 4, core: 2. Of those that a mesh axis runs over, the one named last changes fastest.
Arguments:
- tiles: bfloat16 [4, 8, 6, 256, 256], P('band', 'roster'), as said below
- tile_slots: int32 [4, 8, 6], P('band', 'roster'), may hold values from 0 to 5, each once within a row
- tile_count: int32 [4, 8], P('band', 'roster'), may hold values from 1 to 6, as said below
- costs: float32 [6144, 128], P('roster'), may hold values from 1000 to 10000
- primal_start: float32 [6144, 128], P('roster'), may hold values from 0 to 1
- dual_start: float32 [2048, 128], P('band'), may hold values from 0.5 to 4
Outputs:
- primal: float32 [6144, 128], P('roster')
- dual: float32 [2048, 128], P('band')
Inputs may be any that keep to these rules, and one draw needn't show every extreme that they name: `tile_slots`: each device's slots list every tile position once; slot s is in use where s < tile_count. `tile_count`: some device uses all 6 slots. `tiles`: entries are zero or positive.
All inputs are finite; a program needn't handle non-finite values.
Results may differ from a plain program's by a relative error of at most 0.0003.
Values sent between devices are 32-bit elements; how exact they have to be, the bound alone decides.
A program may use at most 64 MiB of HBM per device.

v0:
```python
import jax
import jax.numpy as jnp
from jax import lax
from jax.sharding import PartitionSpec as P

ROUNDS = 3
ITERS = 4


HIGH = lax.Precision.HIGHEST
eps = 1e-06


def shards(tiles, tile_slots, tile_count, costs, primal_start, dual_start):
    tile_block = tiles[0, 0]
    slots = tile_slots[0, 0]
    count = tile_count[0, 0]
    tile = tile_block.shape[1]
    rows = dual_start.shape[0]
    cols = costs.shape[0]
    row_tiles = rows // tile
    col_tiles = cols // tile
    row_index = slots // col_tiles
    col_index = slots % col_tiles
    active = (jnp.arange(slots.shape[0], dtype=jnp.int32) < count).astype(jnp.float32)
    row_hot = (row_index[None, :] == jnp.arange(row_tiles, dtype=jnp.int32)[:, None]).astype(
        jnp.float32
    )
    col_hot = (col_index[None, :] == jnp.arange(col_tiles, dtype=jnp.int32)[:, None]).astype(
        jnp.float32
    )

    def scale_tiles(row_scale, col_scale):
        row_part = row_scale.reshape(row_tiles, tile)[row_index]
        col_part = col_scale.reshape(col_tiles, tile)[col_index]
        return (
            tile_block.astype(jnp.float32)
            * row_part[:, :, None]
            * col_part[:, None, :]
            * active[:, None, None]
        )

    row_scale = jnp.ones((rows,), jnp.float32)
    col_scale = jnp.ones((cols,), jnp.float32)
    for turn in range(ROUNDS):
        magnitude = jnp.abs(scale_tiles(row_scale, col_scale))
        slot_rows = jnp.max(magnitude, axis=2)
        slot_cols = jnp.max(magnitude, axis=1)
        row_peak = jnp.max(row_hot[:, :, None] * slot_rows[None], axis=1).reshape(-1)
        col_peak = jnp.max(col_hot[:, :, None] * slot_cols[None], axis=1).reshape(-1)
        row_peak = lax.pmax(row_peak, "roster")
        col_peak = lax.pmax(col_peak, "band")
        row_scale = row_scale / jnp.sqrt(row_peak + eps)
        col_scale = col_scale / jnp.sqrt(col_peak + eps)
    scaled = scale_tiles(row_scale, col_scale)
    squares = lax.psum(jnp.sum(scaled * scaled), ("band", "roster"))
    eta = 0.9 / jnp.sqrt(squares + eps)
    scen = costs.shape[1]
    col_full = col_scale[:, None]
    row_full = row_scale[:, None]
    cost_t = costs * col_full
    upper = 1.0 / col_full
    primal = primal_start / col_full
    dual = dual_start / row_full
    for step in range(ITERS):
        dual_slots = dual.reshape(row_tiles, tile, scen)[row_index]
        back_terms = jnp.einsum("sij,sik->sjk", scaled, dual_slots, precision=HIGH)
        g_local = jnp.einsum("cs,sjk->cjk", col_hot, back_terms, precision=HIGH).reshape(cols, scen)
        g_whole = lax.psum(g_local, "band")
        primal_next = jnp.clip(primal - eta * (cost_t - g_whole), 0.0, upper)
        extrapolated = 2.0 * primal_next - primal
        primal_slots = extrapolated.reshape(col_tiles, tile, scen)[col_index]
        fore_terms = jnp.einsum("sij,sjk->sik", scaled, primal_slots, precision=HIGH)
        h_local = jnp.einsum("rs,sik->rik", row_hot, fore_terms, precision=HIGH).reshape(rows, scen)
        share = rows // lax.axis_size("roster")
        begin = lax.axis_index("roster") * share
        h_share = lax.psum_scatter(h_local, "roster", scatter_dimension=0, tiled=True)
        own_dual = lax.dynamic_slice_in_dim(dual, begin, share, 0)
        own_rows = lax.dynamic_slice_in_dim(row_full, begin, share, 0)
        dual_share = own_dual + eta * (own_rows - h_share)
        dual = lax.all_gather(dual_share, "roster", axis=0, tiled=True)
        primal = primal_next
    return (primal, dual)


def solution(mesh):
    placed = (
        P("band", "roster", None, None, None),
        P("band", "roster", None),
        P("band", "roster"),
        P("roster", None),
        P("roster", None),
        P("band", None),
    )
    return jax.shard_map(
        shards,
        mesh=mesh,
        in_specs=placed,
        out_specs=(P("roster", None), P("band", None)),
        check_vma=False,
    )
```

profile of v0, /device:TPU:0, one launch (start us, length us, event | category | flops | bytes accessed | tf_op | source)
XLA Modules:
  0.0 466.0 jit_solution(17935510203944272796)
XLA Ops:
  10.5 1.8 fusion.3
  12.4 15.1 %pmax.43 = f32[512]{0:T(512)S(1)} all-reduce(f32[512]{0:T(512)S(1)} %bitcast.135), channel_id=1, replica_groups=mesh['band'=4,'roster'=8] {'roster'}, use_global_device_ids=true, to_apply=%region_5.6 | all-reduce | flops 512 | bytes 4096 | tf_op jit(solution)/shard_map/pmax | solution.py:51
  27.7 12.0 %pmax.42 = f32[768]{0:T(1024)S(1)} all-reduce(f32[768]{0:T(1024)S(1)} %reshape.279), channel_id=1, replica_groups=mesh['band'=4,'roster'=8] {'band'}, use_global_device_ids=true, to_apply=%region_2.3 | all-reduce | flops 768 | bytes 6144 | tf_op jit(solution)/shard_map/pmax | solution.py:52
  41.6 8.4 %pmax.44 = f32[768]{0:T(1024)S(1)} all-reduce(f32[768]{0:T(1024)S(1)} %reshape.283), channel_id=1, replica_groups=mesh['band'=4,'roster'=8] {'band'}, use_global_device_ids=true, to_apply=%region_8.9 | all-reduce | flops 768 | bytes 6144 | tf_op jit(solution)/shard_map/pmax | solution.py:52
  50.0 11.8 %pmax.45 = f32[512]{0:T(512)S(1)} all-reduce(f32[512]{0:T(512)S(1)} %bitcast.136), channel_id=1, replica_groups=mesh['band'=4,'roster'=8] {'roster'}, use_global_device_ids=true, to_apply=%region_11.12 | all-reduce | flops 512 | bytes 4096 | tf_op jit(solution)/shard_map/pmax | solution.py:51
  63.8 10.4 %pmax.46 = f32[768]{0:T(1024)S(1)} all-reduce(f32[768]{0:T(1024)S(1)} %reshape.287), channel_id=1, replica_groups=mesh['band'=4,'roster'=8] {'band'}, use_global_device_ids=true, to_apply=%region_14.15 | all-reduce | flops 768 | bytes 6144 | tf_op jit(solution)/shard_map/pmax | solution.py:52
  74.2 11.8 %pmax.47 = f32[512]{0:T(512)S(1)} all-reduce(f32[512]{0:T(512)S(1)} %bitcast.137), channel_id=1, replica_groups=mesh['band'=4,'roster'=8] {'roster'}, use_global_device_ids=true, to_apply=%region_17.18 | all-reduce | flops 512 | bytes 4096 | tf_op jit(solution)/shard_map/pmax | solution.py:51
  87.9 2.9 fusion.31
  93.9 37.9 %psum.35 = f32[]{:T(128)} all-reduce(f32[]{:T(128)} %fusion.34), channel_id=1, replica_groups=mesh['band'=4,'roster'=8] {'band','roster'}, use_global_device_ids=true, to_apply=%region_19.20 | all-reduce | flops 1 | bytes 8 | tf_op jit(solution)/shard_map/psum | solution.py:56
  138.2 33.9 %reduce-scatter.5.cloned.1.call-done = f32[64,128]{1,0:T(8,128)} async-done(((f32[512,128]{1,0:T(8,128)}), f32[64,128]{1,0:T(8,128)}) %reduce-scatter.5.cloned.1.call-update) | async-done | bytes 32784 | tf_op jit(solution)/shard_map/reduce_scatter | solution.py:77
  172.8 9.4 %all_gather.12 = f32[512,128]{1,0:T(8,128)S(1)} all-gather(f32[64,128]{1,0:T(8,128)S(1)} %multiply_add_fusion.3), channel_id=1, replica_groups=mesh['band'=4,'roster'=8] {'roster'}, dimensions={0}, use_global_device_ids=true | all-gather | bytes 294912 | tf_op jit(solution)/shard_map/all_gather | solution.py:81
  182.9 3.0 fusion.27
  187.7 37.0 %all-reduce.7.cloned.1.call-done = f32[768,128]{1,0:T(8,128)} async-done(((f32[768,128]{1,0:T(8,128)}), f32[768,128]{1,0:T(8,128)}) %all-reduce.7.cloned.1.call-update) | async-done | bytes 393232 | tf_op jit(solution)/shard_map/psum | solution.py:69
  230.1 33.5 %reduce-scatter.7.cloned.1.call-done = f32[64,128]{1,0:T(8,128)} async-done(((f32[512,128]{1,0:T(8,128)}), f32[64,128]{1,0:T(8,128)}) %reduce-scatter.7.cloned.1.call-update) | async-done | bytes 32784 | tf_op jit(solution)/shard_map/reduce_scatter | solution.py:77
  264.5 9.4 %all_gather.13 = f32[512,128]{1,0:T(8,128)S(1)} all-gather(f32[64,128]{1,0:T(8,128)S(1)} %multiply_add_fusion.2), channel_id=1, replica_groups=mesh['band'=4,'roster'=8] {'roster'}, dimensions={0}, use_global_device_ids=true | all-gather | bytes 294912 | tf_op jit(solution)/shard_map/all_gather | solution.py:81
  274.6 2.9 fusion.23
  279.4 37.1 %all-reduce.9.cloned.1.call-done = f32[768,128]{1,0:T(8,128)} async-done(((f32[768,128]{1,0:T(8,128)}), f32[768,128]{1,0:T(8,128)}) %all-reduce.9.cloned.1.call-update) | async-done | bytes 393232 | tf_op jit(solution)/shard_map/psum | solution.py:69
  321.9 33.5 %reduce-scatter.9.cloned.1.call-done = f32[64,128]{1,0:T(8,128)} async-done(((f32[512,128]{1,0:T(8,128)}), f32[64,128]{1,0:T(8,128)}) %reduce-scatter.9.cloned.1.call-update) | async-done | bytes 32784 | tf_op jit(solution)/shard_map/reduce_scatter | solution.py:77
  356.3 9.5 %all_gather.14 = f32[512,128]{1,0:T(8,128)S(1)} all-gather(f32[64,128]{1,0:T(8,128)S(1)} %multiply_add_fusion.1), channel_id=1, replica_groups=mesh['band'=4,'roster'=8] {'roster'}, dimensions={0}, use_global_device_ids=true | all-gather | bytes 294912 | tf_op jit(solution)/shard_map/all_gather | solution.py:81
  366.3 2.9 fusion.19
  371.1 37.1 %all-reduce.11.cloned.1.call-done = f32[768,128]{1,0:T(8,128)} async-done(((f32[768,128]{1,0:T(8,128)}), f32[768,128]{1,0:T(8,128)}) %all-reduce.11.cloned.1.call-update) | async-done | bytes 393232 | tf_op jit(solution)/shard_map/psum | solution.py:69
  408.2 2.0 multiply_subtract_fusion
  414.3 33.6 %reduce-scatter.11.cloned.1.call-done = f32[64,128]{1,0:T(8,128)} async-done(((f32[512,128]{1,0:T(8,128)}), f32[64,128]{1,0:T(8,128)}) %reduce-scatter.11.cloned.1.call-update) | async-done | bytes 32784 | tf_op jit(solution)/shard_map/reduce_scatter | solution.py:77
  448.8 9.2 %all_gather.15 = f32[512,128]{1,0:T(8,128)S(1)} all-gather(f32[64,128]{1,0:T(8,128)S(1)} %multiply_add_fusion), channel_id=1, replica_groups=mesh['band'=4,'roster'=8] {'roster'}, dimensions={0}, use_global_device_ids=true | all-gather | bytes 294912 | tf_op jit(solution)/shard_map/all_gather | solution.py:81
  (107 shorter events, 43.4 us)
Async XLA Ops:
  7.2 33.6 %copy-start = (bf16[1,1,6,256,256]{4,3,2,1,0:T(8,128)(2,1)S(1)}, bf16[1,1,6,256,256]{4,3,2,1,0:T(8,128)(2,1)}, u32[]{:S(2)}) copy-start(bf16[1,1,6,256,256]{4,3,2,1,0:T(8,128)(2,1)} %param.6) | copy-start | bytes 2359300
  7.2 125.4 %all-reduce.5.cloned.1.call-start = ((), (), s32[]{:S(2)}) async-start(), calls=%async_computation.4 | async-start | bytes 786432 | tf_op jit(solution)/shard_map/psum | solution.py:69
  41.4 45.7 %copy-start.3 = (f32[512,128]{1,0:T(8,128)S(1)}, f32[512,128]{1,0:T(8,128)}, u32[]{:S(2)}) copy-start(f32[512,128]{1,0:T(8,128)} %param.11) | copy-start | bytes 786436
  92.7 39.9 %copy-start.1 = (f32[768,128]{1,0:T(8,128)S(1)}, f32[768,128]{1,0:T(8,128)}, u32[]{:S(2)}) copy-start(f32[768,128]{1,0:T(8,128)} %param.9) | copy-start | bytes 1179652
  92.7 39.9 %copy-start.2 = (f32[768,128]{1,0:T(8,128)S(1)}, f32[768,128]{1,0:T(8,128)}, u32[]{:S(2)}) copy-start(f32[768,128]{1,0:T(8,128)} %param.10) | copy-start | bytes 1179652
  92.7 79.3 %reduce-scatter.5.cloned.1.call-start = ((), (), s32[]{:S(2)}) async-start(), calls=%async_computation.5 | async-start | bytes 294912 | tf_op jit(solution)/shard_map/reduce_scatter | solution.py:77
  138.0 86.7 %all-reduce.7.cloned.1.call-start = ((), (), s32[]{:S(2)}) async-start(), calls=%async_computation.6 | async-start | bytes 786432 | tf_op jit(solution)/shard_map/psum | solution.py:69
  187.6 76.1 %reduce-scatter.7.cloned.1.call-start = ((), (), s32[]{:S(2)}) async-start(), calls=%async_computation.7 | async-start | bytes 294912 | tf_op jit(solution)/shard_map/reduce_scatter | solution.py:77
  230.1 86.3 %all-reduce.9.cloned.1.call-start = ((), (), s32[]{:S(2)}) async-start(), calls=%async_computation.8 | async-start | bytes 786432 | tf_op jit(solution)/shard_map/psum | solution.py:69
  279.3 76.1 %reduce-scatter.9.cloned.1.call-start = ((), (), s32[]{:S(2)}) async-start(), calls=%async_computation.9 | async-start | bytes 294912 | tf_op jit(solution)/shard_map/reduce_scatter | solution.py:77
  321.8 86.4 %all-reduce.11.cloned.1.call-start = ((), (), s32[]{:S(2)}) async-start(), calls=%async_computation.10 | async-start | bytes 786432 | tf_op jit(solution)/shard_map/psum | solution.py:69
  371.1 76.8 %reduce-scatter.11.cloned.1.call-start = ((), (), s32[]{:S(2)}) async-start(), calls=%async_computation.11 | async-start | bytes 294912 | tf_op jit(solution)/shard_map/reduce_scatter | solution.py:77
Sparse Core Ops, SparseCore 0:
  92.8 33.2 all-reduce.4
  138.1 33.8 reduce-scatter.4
  187.7 36.9 all-reduce.6
  230.2 33.4 reduce-scatter.6
  279.4 36.9 all-reduce.8
  321.9 33.4 reduce-scatter.8
  371.2 36.9 all-reduce.10
  414.5 33.4 reduce-scatter.10
where the time goes:
time: 475 us; the launch traced here: 466 us
  waiting for transfers between devices  246 us (52%)
  blocking collectives  145 us (31%)
  matrix products  26.8 us (6%)
  local copies, waits for them, and re-layouts  16.3 us (3%)
  between operations  16.3 us (3%)
  other arithmetic  15.4 us (3%)
    reduce_scatter x4, waiting for transfers between devices, shards(): lax.psum_scatter(h_local, 'roster', scatter_dimension=0, tiled=True)  135 us
    psum x4, waiting for transfers between devices, shards(): g_whole = lax.psum(g_local, 'band')  111 us
    pmax x3, blocking collectives, shards(): row_peak = lax.pmax(row_peak, 'roster')  38.7 us
    psum x1, blocking collectives, shards(): squares = lax.psum(jnp.sum(scaled * scaled), ('band', 'roster'))  37.9 us
    all_gather x4, blocking collectives, shards(): dual = lax.all_gather(dual_share, 'roster', axis=0, tiled=True)  37.6 us
    pmax x3, blocking collectives, shards(): col_peak = lax.pmax(col_peak, 'band')  30.7 us
    dot_general x4, matrix products, shards(): back_terms = jnp.einsum('sij,sik->sjk', scaled, dual_slots, precision=HIGH)  11.8 us
  transfers between devices with their start and end apart: 8, of which 7 were waited for; matrix products, arithmetic and copies ran while one was open for 0% of the time, Pallas kernels for 0%

commit v1 on v0

v1 whole, which is shorter than its diff:
```python
import functools

import jax
import jax.numpy as jnp
from jax import lax
from jax.experimental import pallas as pl
from jax.experimental.pallas import tpu as pltpu
from jax.sharding import PartitionSpec as P

ROUNDS = 3
ITERS = 4
eps = 1e-06
GROUPS = 1
CHUNK = 16
SKEW = 2
DOWN = 2.0**-24
UP = 2.0**24
MESH = pl.DeviceIdType.MESH
f32 = jnp.float32
bf16 = jnp.bfloat16


def kernel(
    cfg, slots_ref, count_ref, tiles_ref, cost_ref, x0_ref, y0_ref, primal_ref, dual_ref,
    a_ref, at_ref, cost_t, x_t, u_t, y_t, own, snd, rec, hown, hrec,
    rpeak_s, rpeak_r, cpeak_s, cpeak_r, fr_s, fr_r, fb_s, fb_r,
    rp_ss, rp_rs, cp_ss, cp_rs, fr_ss, fr_rs, fb_ss, fb_rs,
    g_ss, g_rs, rs_ss, rs_rs, ag_ss, ag_rs,
):
    nb, nr, groups, cs, skew = cfg
    z = lax.axis_index("band")
    r = lax.axis_index("roster")
    slots = tiles_ref.shape[2]
    tile = tiles_ref.shape[3]
    rows, scen = y0_ref.shape
    cols = cost_ref.shape[0]
    col_tiles = cols // tile
    per = scen // groups
    kper = per // cs
    bs = max(8, per // nr)
    width = per * rows // (nr * bs)
    parts = rows // width

    def roster_peer(d):
        return (z, (r + d) % nr)

    def band_peer(d):
        return ((z + d) % nb, r)

    barrier = pltpu.get_barrier_semaphore()
    for d in range(1, nr):
        pl.semaphore_signal(barrier, inc=1, device_id=roster_peer(d), device_id_type=MESH)
    for d in range(1, nb):
        pl.semaphore_signal(barrier, inc=1, device_id=band_peer(d), device_id_type=MESH)

    for p in range(slots):
        at = jnp.int32(0)
        for s in range(slots):
            at = jnp.where(slots_ref[0, 0, s] == p, jnp.int32(s), at)
        factor = jnp.where(at < count_ref[0, 0], jnp.float32(DOWN), jnp.float32(0.0))
        block = tiles_ref[0, 0, at].astype(f32) * factor
        i, j = (p // col_tiles) * tile, (p % col_tiles) * tile
        a_ref[i : i + tile, j : j + tile] = block.astype(bf16)
        at_ref[j : j + tile, i : i + tile] = block.T.astype(bf16)

    def fold(ref, at, factor, op):
        part = ref[at : at + 128, :].astype(f32) * factor
        if op is jnp.add:
            part = part * part
        total = part[:, :128]
        for j in range(128, part.shape[1], 128):
            total = op(total, part[:, j : j + 128])
        return total.T

    def peaks(turn, row, col_up):
        for i in range(0, rows, 128):
            peak = jnp.max(fold(a_ref, i, col_up, jnp.maximum), axis=0, keepdims=True)
            rpeak_s[turn, :, i : i + 128] = peak * row[:, i : i + 128]
        for j in range(0, cols, 128):
            peak = jnp.max(fold(at_ref, j, row, jnp.maximum), axis=0, keepdims=True)
            cpeak_s[turn, :, j : j + 128] = peak * col_up[:, j : j + 128]

    def rpeak_copy(turn, d):
        return pltpu.make_async_remote_copy(
            rpeak_s.at[turn], rpeak_r.at[turn, d], rp_ss.at[turn, d], rp_rs.at[turn, d],
            device_id=roster_peer(d), device_id_type=MESH)

    def cpeak_copy(turn, d):
        return pltpu.make_async_remote_copy(
            cpeak_s.at[turn], cpeak_r.at[turn, d], cp_ss.at[turn, d], cp_rs.at[turn, d],
            device_id=band_peer(d), device_id_type=MESH)

    def peaks_send(turn):
        for d in range(1, nb):
            cpeak_copy(turn, d).start()
        for d in range(1, nr):
            rpeak_copy(turn, d).start()

    def peaks_wait(turn):
        row = rpeak_s[turn]
        col = cpeak_s[turn]
        for d in range(1, nr):
            rpeak_copy(turn, d).wait_recv()
            row = jnp.maximum(row, rpeak_r[turn, d])
        for d in range(1, nb):
            cpeak_copy(turn, d).wait_recv()
            col = jnp.maximum(col, cpeak_r[turn, d])
        return row, col

    def fr_copy(d):
        return pltpu.make_async_remote_copy(
            fr_s, fr_r.at[d], fr_ss.at[d], fr_rs.at[d],
            device_id=roster_peer(d), device_id_type=MESH)

    def fb_copy(d):
        return pltpu.make_async_remote_copy(
            fb_s, fb_r.at[d], fb_ss.at[d], fb_rs.at[d],
            device_id=band_peer(d), device_id_type=MESH)

    is_end = (z == 0) | (z == nb - 1)
    inner = (z > 0) & (z < nb - 1)
    lead = (z * 2) // nb
    back = 1 - lead

    def split_dot(value, matrix):
        high = value.astype(bf16)
        low = (value - high.astype(f32)).astype(bf16)
        both = jnp.dot(jnp.concatenate([high, low], 0), matrix, preferred_element_type=f32)
        return both[: value.shape[0]] + both[value.shape[0] :]

    def g_copy(par, way, k):
        at = pl.ds(k * cs, cs)
        return pltpu.make_async_remote_copy(
            snd.at[way, at], rec.at[par, way, at], g_ss.at[way, k], g_rs.at[par, way, k],
            device_id=((z + nb + 1 - 2 * way) % nb, r), device_id_type=MESH)

    def g_sent(grp, par):
        for k in range(grp * kper, (grp + 1) * kper):
            g_copy(par, lead, k).wait_send()

        @pl.when(inner)
        def _():
            for k in range(grp * kper, (grp + 1) * kper):
                g_copy(par, back, k).wait_send()

    def g_start(grp, t):
        if t > 0:
            g_sent(grp, (t - 1) % 2)
        at = pl.ds(grp * per, per)
        value = split_dot(y_t[at, :], a_ref[...])
        own[at, :] = value

        @pl.when(is_end)
        def _():
            snd[lead, at, :] = value
            for k in range(grp * kper, (grp + 1) * kper):
                g_copy(t % 2, lead, k).start()

    def first(t, k):
        @pl.when(inner)
        def _():
            at = pl.ds(k * cs, cs)
            g_copy(t % 2, lead, k).wait_recv()
            snd[lead, at, :] = rec[t % 2, lead, at, :] + own[at, :]
            g_copy(t % 2, lead, k).start()

    def second(t, k):
        g_copy(t % 2, back, k).wait_recv()

        @pl.when(inner)
        def _():
            at = pl.ds(k * cs, cs)
            snd[back, at, :] = rec[t % 2, back, at, :] + own[at, :]
            g_copy(t % 2, back, k).start()

    def block_at(grp, q):
        if parts == 1:
            return (pl.ds(pl.multiple_of(grp * per + q * bs, 8), bs), slice(None))
        return (
            pl.ds(pl.multiple_of(grp * per + (q // parts) * bs, 8), bs),
            pl.ds(pl.multiple_of((q % parts) * width, 128), width),
        )

    def rs_copy(grp, d):
        return pltpu.make_async_remote_copy(
            hown.at[block_at(grp, (r + d) % nr)], hrec.at[grp, d],
            rs_ss.at[grp, d], rs_rs.at[grp, d],
            device_id=roster_peer(d), device_id_type=MESH)

    def ag_copy(grp, d):
        here = block_at(grp, r)
        return pltpu.make_async_remote_copy(
            y_t.at[here], y_t.at[here], ag_ss.at[grp, d], ag_rs.at[grp, d],
            device_id=roster_peer(d), device_id_type=MESH)

    def ag_arrived(grp, d):
        here = block_at(grp, (r + nr - d) % nr)
        return pltpu.make_async_remote_copy(
            y_t.at[here], y_t.at[here], ag_ss.at[grp, d], ag_rs.at[grp, d],
            device_id=roster_peer(d), device_id_type=MESH)

    order = sorted(range(1, nr), key=lambda d: -bin(d).count("1"))

    one_row = jnp.ones((1, rows), f32)
    one_col = jnp.ones((1, cols), f32)
    row, col_up = one_row, one_col * UP
    peaks(0, row, col_up)
    pl.semaphore_wait(barrier, nr - 1 + nb - 1)
    peaks_send(0)
    for i in range(0, rows, 128):
        y_t[:, i : i + 128] = y0_ref[i : i + 128, :].T
    for grp in range(groups):
        g_start(grp, 0)

    steps = []
    for k in range(groups * kper + skew):
        if k < groups * kper:
            steps.append(functools.partial(first, 0, k))
        if k >= skew:
            steps.append(functools.partial(second, 0, k - skew))
    take = -(-len(steps) // (ROUNDS + 1))
    for turn in range(ROUNDS):
        if turn == 0:
            for j in range(0, cols, 128):
                cost_t[:, j : j + 128] = cost_ref[j : j + 128, :].T
                x_t[:, j : j + 128] = x0_ref[j : j + 128, :].T
        for step in steps[turn * take : (turn + 1) * take]:
            step()
        row_peak, col_peak = peaks_wait(turn)
        row = row / jnp.sqrt(row_peak + eps)
        col_up = col_up / jnp.sqrt(col_peak + eps)
        if turn + 1 < ROUNDS:
            peaks(turn + 1, row, col_up)
            peaks_send(turn + 1)
    col = col_up * DOWN
    row_up = row * UP

    squares = jnp.zeros((1, 128), f32)
    for j in range(0, cols, 128):
        part = jnp.sum(fold(at_ref, j, row, jnp.add), axis=0, keepdims=True)
        scale = col_up[:, j : j + 128]
        squares = squares + part * scale * scale
    fr_s[...] = squares
    for d in range(1, nr):
        fr_copy(d).start()
    for j in range(0, cols, 128):
        cost_t[:, j : j + 128] = cost_t[:, j : j + 128] * col[:, j : j + 128]
    for d in range(1, nr):
        fr_copy(d).wait_recv()
        squares = squares + fr_r[d]
    fb_s[...] = squares
    for d in range(1, nb):
        fb_copy(d).start()
    for step in steps[ROUNDS * take :]:
        step()
    for d in range(1, nb):
        fb_copy(d).wait_recv()
        squares = squares + fb_r[d]
    eta = 0.9 / jnp.sqrt(jnp.sum(squares, axis=1, keepdims=True) + eps)
    eta_col = eta * col
    eta_row = eta * row

    def update(t, k):
        at = pl.ds(k * cs, cs)
        total = snd[lead, at, :] + rec[t % 2, back, at, :]
        before = x_t[at, :]
        after = jnp.clip(before - eta_col * (cost_t[at, :] - col_up * total), 0.0, 1.0)
        x_t[at, :] = after
        u_t[at, :] = 2.0 * after - before

    def h_start(grp, t):
        if t > 0:
            for d in order:
                rs_copy(grp, d).wait_send()
        at = pl.ds(grp * per, per)
        hown[at, :] = split_dot(u_t[at, :], at_ref[...])
        for d in order:
            rs_copy(grp, d).start()

    def h_mid(grp, t):
        here = block_at(grp, r)
        total = hown[here]
        for d in range(1, nr):
            rs_copy(grp, d).wait_recv()
            total = total + hrec[grp, d]
        if t > 0:
            for d in order:
                ag_copy(grp, d).wait_send()
        if parts == 1:
            y_t[here] = y_t[here] + eta_row * (row - row_up * total)
        else:
            lane = (r % parts) * width
            own_row = jnp.zeros((1, width), f32)
            own_eta = jnp.zeros((1, width), f32)
            for q in range(parts):
                mine = lane == q * width
                own_row = jnp.where(mine, row[:, q * width : (q + 1) * width], own_row)
                own_eta = jnp.where(mine, eta_row[:, q * width : (q + 1) * width], own_eta)
            y_t[here] = y_t[here] + own_eta * (own_row - (own_row * UP) * total)
        for d in order:
            ag_copy(grp, d).start()

    def h_fin(grp):
        for d in range(1, nr):
            ag_arrived(grp, d).wait_recv()

    def relays(t, grp, lo, hi):
        for k in range(lo, hi):
            if k < kper:
                first(t, grp * kper + k)
            if k >= skew:
                second(t, grp * kper + k - skew)
                update(t, grp * kper + k - skew)

    for t in range(ITERS):
        if t == 0:
            for k in range(groups * kper):
                update(0, k)
                if (k + 1) % kper == 0:
                    h_start(k // kper, 0)
            for grp in range(groups):
                h_mid(grp, 0)
        elif groups == 1:
            relays(t, 0, 0, kper + skew)
            h_start(0, t)
            h_mid(0, t)
        else:
            relays(t, 0, 0, kper + skew)
            h_start(0, t)
            relays(t, 1, 0, kper)
            h_mid(0, t)
            relays(t, 1, kper, kper + skew)
            h_start(1, t)
            if t + 1 < ITERS:
                h_fin(0)
                g_start(0, t + 1)
            h_mid(1, t)
        for grp in range(groups):
            if t + 1 == ITERS:
                h_fin(grp)
            elif groups == 1 or t == 0 or grp > 0:
                h_fin(grp)
                g_start(grp, t + 1)

    for j in range(0, cols, 128):
        primal_ref[j : j + 128, :] = (x_t[:, j : j + 128] / col[:, j : j + 128]).T
    for i in range(0, rows, 128):
        dual_ref[i : i + 128, :] = (y_t[:, i : i + 128] / row[:, i : i + 128]).T

    for grp in range(groups):
        g_sent(grp, (ITERS - 1) % 2)
        for d in order:
            rs_copy(grp, d).wait_send()
            ag_copy(grp, d).wait_send()
    for d in range(1, nr):
        fr_copy(d).wait_send()
        for turn in range(ROUNDS):
            rpeak_copy(turn, d).wait_send()
    for d in range(1, nb):
        fb_copy(d).wait_send()
        for turn in range(ROUNDS):
            cpeak_copy(turn, d).wait_send()


def shards(nb, nr, tiles, tile_slots, tile_count, costs, primal_start, dual_start):
    rows, scen = dual_start.shape
    cols = costs.shape[0]
    groups = GROUPS if (scen // GROUPS) * rows // nr >= 1024 else 1
    cs = CHUNK
    chunks = scen // cs
    per = scen // groups
    bs = max(8, per // nr)
    width = per * rows // (nr * bs)
    vmem = pl.BlockSpec(memory_space=pltpu.VMEM)
    smem = pl.BlockSpec(memory_space=pltpu.SMEM)
    dma = pltpu.SemaphoreType.DMA
    return pl.pallas_call(
        functools.partial(kernel, (nb, nr, groups, cs, SKEW)),
        name="primal_dual",
        out_shape=(
            jax.ShapeDtypeStruct((cols, scen), f32),
            jax.ShapeDtypeStruct((rows, scen), f32),
        ),
        in_specs=[smem, smem, vmem, vmem, vmem, vmem],
        out_specs=(vmem, vmem),
        scratch_shapes=[
            pltpu.VMEM((rows, cols), bf16),
            pltpu.VMEM((cols, rows), bf16),
            pltpu.VMEM((scen, cols), f32),
            pltpu.VMEM((scen, cols), f32),
            pltpu.VMEM((scen, cols), f32),
            pltpu.VMEM((scen, rows), f32),
            pltpu.VMEM((scen, cols), f32),
            pltpu.VMEM((2, scen, cols), f32),
            pltpu.VMEM((2, 2, scen, cols), f32),
            pltpu.VMEM((scen, rows), f32),
            pltpu.VMEM((groups, nr, bs, width), f32),
            pltpu.VMEM((ROUNDS, 1, rows), f32),
            pltpu.VMEM((ROUNDS, nr, 1, rows), f32),
            pltpu.VMEM((ROUNDS, 1, cols), f32),
            pltpu.VMEM((ROUNDS, nb, 1, cols), f32),
            pltpu.VMEM((1, 128), f32),
            pltpu.VMEM((nr, 1, 128), f32),
            pltpu.VMEM((1, 128), f32),
            pltpu.VMEM((nb, 1, 128), f32),
            dma((ROUNDS, nr)),
            dma((ROUNDS, nr)),
            dma((ROUNDS, nb)),
            dma((ROUNDS, nb)),
            dma((nr,)),
            dma((nr,)),
            dma((nb,)),
            dma((nb,)),
            dma((2, chunks)),
            dma((2, 2, chunks)),
            dma((groups, nr)),
            dma((groups, nr)),
            dma((groups, nr)),
            dma((groups, nr)),
        ],
        compiler_params=pltpu.CompilerParams(collective_id=0, has_side_effects=True),
    )(tile_slots, tile_count, tiles, costs, primal_start, dual_start)


def solution(mesh):
    placed = (
        P("band", "roster", None, None, None),
        P("band", "roster", None),
        P("band", "roster"),
        P("roster", None),
        P("roster", None),
        P("band", None),
    )
    return jax.shard_map(
        functools.partial(shards, mesh.shape["band"], mesh.shape["roster"]),
        mesh=mesh,
        in_specs=placed,
        out_specs=(P("roster", None), P("band", None)),
        check_vma=False,
    )
```

time: 475 us -> 131 us (0.28); the launches traced: 466 us -> 131 us
  waiting for transfers between devices: 246 us -> 0 us
  blocking collectives: 145 us -> 0 us
  Pallas kernels: 0 us -> 127 us
  matrix products: 26.8 us -> 0 us
  other arithmetic: 15.4 us -> 0 us
  between operations: 16.3 us -> 1.29 us
  local copies, waits for them, and re-layouts: 16.3 us -> 2.52 us
    reduce_scatter x4 -> x0, waiting for transfers between devices: 135 us -> none  [shards(): lax.psum_scatter(h_local, 'roster', scatter_dimension=0, tiled=True)]
    pallas_call x0 -> x1, Pallas kernels: none -> 127 us  [shards(): pl.pallas_call(functools.partial(kernel, (nb, nr, groups, cs, SKEW)), nam...]
    psum x4 -> x0, waiting for transfers between devices: 111 us -> none  [shards(): g_whole = lax.psum(g_local, 'band')]
    pmax x6 -> x0, blocking collectives: 69.5 us -> none  [the longest x3 38.7 us: shards(): row_peak = lax.pmax(row_peak, 'roster')]
    psum x1 -> x0, blocking collectives: 37.9 us -> none  [shards(): squares = lax.psum(jnp.sum(scaled * scaled), ('band', 'roster'))]
    all_gather x4 -> x0, blocking collectives: 37.6 us -> none  [shards(): dual = lax.all_gather(dual_share, 'roster', axis=0, tiled=True)]
    dot_general x16 -> x0, matrix products: 26.8 us -> none  [the longest x4 11.8 us: shards(): back_terms = jnp.einsum('sij,sik->sjk', scaled, dual_slots, precision=HIGH)]
    gather x16 -> x0, local copies, waits for them, and re-layouts: 9.28 us -> none  [the longest x4 2.39 us: shards(): primal_slots = extrapolated.reshape(col_tiles, tile, scen)[col_index]]
  transfers between devices with their start and end apart: 8 -> 0, of which waited for: 7 -> 0; matrix products, arithmetic and copies ran while one was open for 0% -> 0% of each run, Pallas kernels for 0% -> 0%
where the time goes in v1:
time: 131 us
  Pallas kernels  127 us (97%)
  local copies, waits for them, and re-layouts  2.52 us (2%)
    pallas_call x1, Pallas kernels, shards(): pl.pallas_call(functools.partial(kernel, (nb, nr, groups, cs, SKEW)), nam...  127 us

profile of v1, /device:TPU:0, one launch (start us, length us, event | category | flops | bytes accessed | tf_op | source)
XLA Modules:
  0.0 130.9 jit_solution(1885980427776426571)
XLA Ops:
  1.3 127.1 %primal_dual.1 = (f32[768,128]{1,0:T(8,128)}, f32[512,128]{1,0:T(8,128)}) custom-call(s32[1,1,6]{2,1,0:T(1,128)} %slots_ref.1, s32[1,1]{1,0:T(1,128)S(6)} %copy.10.count_ref, bf16[1,1,6,256,256]{4,3,2,1,0:T(8,128)(2,1)} %tiles_ref.1, f32[768,128]{1,0:T(8,128)} %cost_ref.1, f32[768,128]{1,0:T(8,128)} %x0_ref.1, f32[512,128]{1,0:T(8,128)} %y0_ref.1), custom_call_target="tpu_custom_call" | custom-call | tf_op jit(solution)/shard_map/primal_dual/pallas_call | solution.py:377
  128.3 0.0 copy-start
  128.4 1.8 %copy.11 = f32[768,128]{1,0:T(8,128)} copy(f32[768,128]{1,0:T(8,128)} %get-tuple-element.4) | data formatting | bytes 786432
  130.2 0.0 copy-done
  130.2 0.7 copy.12
Async XLA Ops:
  128.3 1.8 %copy-start = (f32[512,128]{1,0:T(8,128)S(1)}, f32[512,128]{1,0:T(8,128)}, u32[]{:S(2)}) copy-start(f32[512,128]{1,0:T(8,128)} %get-tuple-element.5) | copy-start | bytes 786436

commit v2 on v1

--- a/solution.py
+++ b/solution.py
@@ -10,9 +10,15 @@
 ROUNDS = 3
 ITERS = 4
 eps = 1e-06
-GROUPS = 1
+GROUPS = 2
 CHUNK = 16
-SKEW = 2
+HOP = 1.7
+LINK = 0.066
+SUM = 4.4
+START = 0.7
+ROUND = 2.0
+FROB = 6.0
+SHIFT = 4.3
 DOWN = 2.0**-24
 UP = 2.0**24
 MESH = pl.DeviceIdType.MESH
@@ -27,7 +33,7 @@
     rp_ss, rp_rs, cp_ss, cp_rs, fr_ss, fr_rs, fb_ss, fb_rs,
     g_ss, g_rs, rs_ss, rs_rs, ag_ss, ag_rs,
 ):
-    nb, nr, groups, cs, skew = cfg
+    nb, nr, groups, cs = cfg
     z = lax.axis_index("band")
     r = lax.axis_index("roster")
     slots = tiles_ref.shape[2]
@@ -212,58 +218,62 @@
     for grp in range(groups):
         g_start(grp, 0)
 
-    steps = []
-    for k in range(groups * kper + skew):
-        if k < groups * kper:
-            steps.append(functools.partial(first, 0, k))
-        if k >= skew:
-            steps.append(functools.partial(second, 0, k - skew))
-    take = -(-len(steps) // (ROUNDS + 1))
-    for turn in range(ROUNDS):
+    state = dict(row=row, col_up=col_up)
+
+    def equilibrate(turn):
         if turn == 0:
             for j in range(0, cols, 128):
                 cost_t[:, j : j + 128] = cost_ref[j : j + 128, :].T
                 x_t[:, j : j + 128] = x0_ref[j : j + 128, :].T
-        for step in steps[turn * take : (turn + 1) * take]:
-            step()
         row_peak, col_peak = peaks_wait(turn)
-        row = row / jnp.sqrt(row_peak + eps)
-        col_up = col_up / jnp.sqrt(col_peak + eps)
+        state["row"] = state["row"] / jnp.sqrt(row_peak + eps)
+        state["col_up"] = state["col_up"] / jnp.sqrt(col_peak + eps)
         if turn + 1 < ROUNDS:
-            peaks(turn + 1, row, col_up)
+            peaks(turn + 1, state["row"], state["col_up"])
             peaks_send(turn + 1)
-    col = col_up * DOWN
-    row_up = row * UP
-
-    squares = jnp.zeros((1, 128), f32)
-    for j in range(0, cols, 128):
-        part = jnp.sum(fold(at_ref, j, row, jnp.add), axis=0, keepdims=True)
-        scale = col_up[:, j : j + 128]
-        squares = squares + part * scale * scale
-    fr_s[...] = squares
-    for d in range(1, nr):
-        fr_copy(d).start()
-    for j in range(0, cols, 128):
-        cost_t[:, j : j + 128] = cost_t[:, j : j + 128] * col[:, j : j + 128]
-    for d in range(1, nr):
-        fr_copy(d).wait_recv()
-        squares = squares + fr_r[d]
-    fb_s[...] = squares
-    for d in range(1, nb):
-        fb_copy(d).start()
-    for step in steps[ROUNDS * take :]:
-        step()
-    for d in range(1, nb):
-        fb_copy(d).wait_recv()
-        squares = squares + fb_r[d]
-    eta = 0.9 / jnp.sqrt(jnp.sum(squares, axis=1, keepdims=True) + eps)
-    eta_col = eta * col
-    eta_row = eta * row
+        else:
+            squares_start()
+
+    def squares_start():
+        row, col_up = state["row"], state["col_up"]
+        col = state["col"] = col_up * DOWN
+        state["row_up"] = row * UP
+        squares = jnp.zeros((1, 128), f32)
+        for j in range(0, cols, 128):
+            part = jnp.sum(fold(at_ref, j, row, jnp.add), axis=0, keepdims=True)
+            scale = col_up[:, j : j + 128]
+            squares = squares + part * scale * scale
+        fr_s[...] = squares
+        for d in range(1, nr):
+            fr_copy(d).start()
+        for j in range(0, cols, 128):
+            cost_t[:, j : j + 128] = cost_t[:, j : j + 128] * col[:, j : j + 128]
+        state["squares"] = squares
+
+    def squares_mid():
+        squares = state["squares"]
+        for d in range(1, nr):
+            fr_copy(d).wait_recv()
+            squares = squares + fr_r[d]
+        fb_s[...] = squares
+        for d in range(1, nb):
+            fb_copy(d).start()
+        state["squares"] = squares
+
+    def squares_end():
+        squares = state["squares"]
+        for d in range(1, nb):
+            fb_copy(d).wait_recv()
+            squares = squares + fb_r[d]
+        eta = 0.9 / jnp.sqrt(jnp.sum(squares, axis=1, keepdims=True) + eps)
+        state["eta_col"] = eta * state["col"]
+        state["eta_row"] = eta * state["row"]
 
     def update(t, k):
         at = pl.ds(k * cs, cs)
         total = snd[lead, at, :] + rec[t % 2, back, at, :]
         before = x_t[at, :]
+        eta_col, col_up = state["eta_col"], state["col_up"]
         after = jnp.clip(before - eta_col * (cost_t[at, :] - col_up * total), 0.0, 1.0)
         x_t[at, :] = after
         u_t[at, :] = 2.0 * after - before
@@ -279,6 +289,7 @@
 
     def h_mid(grp, t):
         here = block_at(grp, r)
+        row, row_up, eta_row = state["row"], state["row_up"], state["eta_row"]
         total = hown[here]
         for d in range(1, nr):
             rs_copy(grp, d).wait_recv()
@@ -304,43 +315,42 @@
         for d in range(1, nr):
             ag_arrived(grp, d).wait_recv()
 
-    def relays(t, grp, lo, hi):
-        for k in range(lo, hi):
-            if k < kper:
-                first(t, grp * kper + k)
-            if k >= skew:
-                second(t, grp * kper + k - skew)
-                update(t, grp * kper + k - skew)
-
-    for t in range(ITERS):
-        if t == 0:
-            for k in range(groups * kper):
-                update(0, k)
-                if (k + 1) % kper == 0:
-                    h_start(k // kper, 0)
-            for grp in range(groups):
-                h_mid(grp, 0)
-        elif groups == 1:
-            relays(t, 0, 0, kper + skew)
-            h_start(0, t)
-            h_mid(0, t)
-        else:
-            relays(t, 0, 0, kper + skew)
-            h_start(0, t)
-            relays(t, 1, 0, kper)
-            h_mid(0, t)
-            relays(t, 1, kper, kper + skew)
-            h_start(1, t)
+    plan = []
+
+    def put(when, step, *args):
+        plan.append((when, len(plan), functools.partial(step, *args)))
+
+    unit = LINK * cs
+    for turn in range(ROUNDS):
+        put(ROUND * (turn + 1), equilibrate, turn)
+    put(ROUND * ROUNDS + FROB / 2, squares_mid)
+    ready = ROUND * ROUNDS + FROB
+    put(ready, squares_end)
+    for grp in range(groups):
+        ks = range(grp * kper, (grp + 1) * kper)
+        for k in ks:
+            put(START + unit * (k + 1) + HOP, first, 0, k)
+            put(START + unit * (k + 2) + 2 * HOP, second, 0, k)
+        begin = max(ready, START + unit * (kper + 2) + 3 * HOP) + grp * SHIFT
+        for t in range(ITERS):
+            if t > 0:
+                for i, k in enumerate(ks):
+                    put(begin + unit * (i + 1) + HOP, first, t, k)
+                    put(begin + unit * (i + 2) + 2 * HOP, second, t, k)
+                    put(begin + unit * (i + 2) + 2 * HOP, update, t, k)
+                begin = begin + unit * (kper + 2) + 3 * HOP
+            else:
+                for k in ks:
+                    put(begin, update, t, k)
+            put(begin, h_start, grp, t)
+            put(begin + SUM, h_mid, grp, t)
+            put(begin + 2 * SUM, h_fin, grp)
             if t + 1 < ITERS:
-                h_fin(0)
-                g_start(0, t + 1)
-            h_mid(1, t)
-        for grp in range(groups):
-            if t + 1 == ITERS:
-                h_fin(grp)
-            elif groups == 1 or t == 0 or grp > 0:
-                h_fin(grp)
-                g_start(grp, t + 1)
+                put(begin + 2 * SUM, g_start, grp, t + 1)
+            begin = begin + 2 * SUM + START
+    for when, index, step in sorted(plan, key=lambda entry: entry[:2]):
+        step()
+    row, col = state["row"], state["col"]
 
     for j in range(0, cols, 128):
         primal_ref[j : j + 128, :] = (x_t[:, j : j + 128] / col[:, j : j + 128]).T
@@ -375,7 +385,7 @@
     smem = pl.BlockSpec(memory_space=pltpu.SMEM)
     dma = pltpu.SemaphoreType.DMA
     return pl.pallas_call(
-        functools.partial(kernel, (nb, nr, groups, cs, SKEW)),
+        functools.partial(kernel, (nb, nr, groups, cs)),
         name="primal_dual",
         out_shape=(
             jax.ShapeDtypeStruct((cols, scen), f32),

time: 131 us -> 119 us (0.908)
  Pallas kernels: 127 us -> 115 us
    pallas_call x1, Pallas kernels: 127 us -> 115 us  [shards(): pl.pallas_call(functools.partial(kernel, (nb, nr, groups, cs)), name='pri...]
where the time goes in v2:
time: 119 us
  Pallas kernels  115 us (97%)
  local copies, waits for them, and re-layouts  2.52 us (2%)
  between operations  1.29 us (1%)
    pallas_call x1, Pallas kernels, shards(): pl.pallas_call(functools.partial(kernel, (nb, nr, groups, cs)), name='pri...  115 us
    unnamed x4, local copies, waits for them, and re-layouts  2.52 us

profile of v2, /device:TPU:0, one launch (start us, length us, event | category | flops | bytes accessed | tf_op | source)
XLA Modules:
  0.0 119.2 jit_solution(11754335222420352801)
XLA Ops:
  1.3 115.4 %primal_dual.1 = (f32[768,128]{1,0:T(8,128)}, f32[512,128]{1,0:T(8,128)}) custom-call(s32[1,1,6]{2,1,0:T(1,128)} %slots_ref.1, s32[1,1]{1,0:T(1,128)S(6)} %copy.10.count_ref, bf16[1,1,6,256,256]{4,3,2,1,0:T(8,128)(2,1)} %tiles_ref.1, f32[768,128]{1,0:T(8,128)} %cost_ref.1, f32[768,128]{1,0:T(8,128)} %x0_ref.1, f32[512,128]{1,0:T(8,128)} %y0_ref.1), custom_call_target="tpu_custom_call" | custom-call | tf_op jit(solution)/shard_map/primal_dual/pallas_call | solution.py:387
  116.7 0.0 copy-start
  116.7 1.8 %copy.11 = f32[768,128]{1,0:T(8,128)} copy(f32[768,128]{1,0:T(8,128)} %get-tuple-element.4) | data formatting | bytes 786432
  118.5 0.0 copy-done
  118.5 0.7 copy.12
Async XLA Ops:
  116.7 1.8 %copy-start = (f32[512,128]{1,0:T(8,128)S(1)}, f32[512,128]{1,0:T(8,128)}, u32[]{:S(2)}) copy-start(f32[512,128]{1,0:T(8,128)} %get-tuple-element.5) | copy-start | bytes 786436
